TPU v7x, 256 devices: a whole 4x4x8 slice. The times are simulated.
256 devices in a mesh: dp: 2 (over z_lo), expert: 128 (over y, x, z_hi, core).
Axes of the slice: x: 4, y: 4, z: 8 (z_hi: 4, z_lo: 2; z = z_hi * 2 + z_lo), core: 2. Of those that a mesh axis runs over, the one named last changes fastest.
Arguments:
- tokens: bfloat16 [32768, 4096], P(('dp', 'expert')), may hold values from -6 to 6
- routes: int32 [256, 16, 4], P(('dp', 'expert')), may hold values from 0 to 127, as said below
- gate_values: float32 [256, 16, 4], P(('dp', 'expert')), may hold values from 0.1 to 1
- gate_weight: bfloat16 [128, 4096, 256], P('expert', 'dp'), may hold values from -0.09375 to 0.09375
- up_weight: bfloat16 [128, 4096, 256], P('expert', 'dp'), may hold values from -0.09375 to 0.09375
- down_weight: bfloat16 [128, 4096, 256], P('expert', 'dp'), may hold values from -0.125 to 0.125
- cotangent: bfloat16 [32768, 4096], P(('dp', 'expert')), may hold values from -6 to 6
Outputs:
- layer_out: bfloat16 [32768, 4096], P(('dp', 'expert'))
- token_grad: bfloat16 [32768, 4096], P(('dp', 'expert'))
- gate_grad: bfloat16 [128, 4096, 256], P('expert', 'dp')
- up_grad: bfloat16 [128, 4096, 256], P('expert', 'dp')
- down_grad: bfloat16 [128, 4096, 256], P('expert', 'dp')
Inputs may be any that keep to these rules, and one draw needn't show every extreme that they name: `routes`: for each home block and each expert, 4 distinct positions within that block.
All inputs are finite; a program needn't handle non-finite values.
Results may differ from a plain program's by a relative error of at most 0.025.
Values may be sent and summed in bfloat16 or wider, within the bound.
A program may use at most 128 MiB of HBM per device.

v0:
```python
import jax
import jax.numpy as jnp
from jax import lax
from jax.sharding import Mesh
from jax.sharding import PartitionSpec as P

SPLIT = 8
ROWS = ("dp", "yx", "col")


def send_out(payload):
    arrived = lax.all_to_all(payload, "yx", split_axis=1, concat_axis=1, tiled=True)
    shared = lax.all_gather(arrived, "col", axis=1, tiled=True)
    return shared.reshape(payload.shape[0], -1, payload.shape[-1])


def bring_back(partial_value, expert_count):
    streams, total_rows, width = partial_value.shape
    summed = lax.psum_scatter(partial_value, "col", scatter_dimension=1, tiled=True)
    summed = summed.reshape(streams, expert_count, -1, width)
    returned = lax.all_to_all(summed, "yx", split_axis=1, concat_axis=1, tiled=True)
    return returned.astype(jnp.float32)


def shards(tokens, routes, gate_values, gate_weight, up_weight, down_weight, cotangent):
    width = tokens.shape[1]
    expert_count = routes.shape[1]
    chosen = routes[0]
    scales = gate_values[0][:, :, None]
    contract_last = (((1,), (1,)), ((), ()))
    contract_first = (((0,), (0,)), ((), ()))
    weights = jnp.concatenate([gate_weight, up_weight, down_weight], axis=0)
    full = lax.all_gather(weights, "dp", axis=1, tiled=True)
    full_gate, full_up, full_down = (full[0], full[1], full[2])
    scaled_cot = (scales * cotangent[chosen].astype(jnp.float32)).astype(jnp.bfloat16)
    both_rows = send_out(jnp.stack([tokens[chosen], scaled_cot]))
    token_rows, cot_rows = (both_rows[0], both_rows[1])
    gate_pre = jnp.dot(token_rows, full_gate, preferred_element_type=jnp.float32)
    up_pre = jnp.dot(token_rows, full_up, preferred_element_type=jnp.float32)
    gate_sigma = jax.nn.sigmoid(gate_pre)
    hidden = (gate_pre * gate_sigma * up_pre).astype(jnp.bfloat16)
    partial_value = lax.dot_general(
        hidden, full_down, contract_last, preferred_element_type=jnp.float32
    ).astype(jnp.bfloat16)
    hidden_grad = jnp.dot(cot_rows, full_down, preferred_element_type=jnp.float32)
    gate_rows = (hidden_grad * up_pre * gate_sigma * (1.0 + gate_pre * (1.0 - gate_sigma))).astype(
        jnp.bfloat16
    )
    up_rows = (hidden_grad * gate_pre * gate_sigma).astype(jnp.bfloat16)
    partial_grad = (
        lax.dot_general(gate_rows, full_gate, contract_last, preferred_element_type=jnp.float32)
        + lax.dot_general(up_rows, full_up, contract_last, preferred_element_type=jnp.float32)
    ).astype(jnp.bfloat16)
    back = bring_back(jnp.stack([partial_value, partial_grad]), expert_count)
    layer_out = jnp.zeros((tokens.shape[0], width), jnp.float32).at[chosen].add(scales * back[0])
    token_grad = jnp.zeros((tokens.shape[0], width), jnp.float32).at[chosen].add(back[1])
    grad_sums = lax.psum_scatter(
        jnp.concatenate(
            [
                lax.dot_general(
                    token_rows, gate_rows, contract_first, preferred_element_type=jnp.float32
                ),
                lax.dot_general(
                    token_rows, up_rows, contract_first, preferred_element_type=jnp.float32
                ),
                lax.dot_general(
                    cot_rows, hidden, contract_first, preferred_element_type=jnp.float32
                ),
            ],
            axis=1,
        ).astype(jnp.bfloat16),
        "dp",
        scatter_dimension=0,
        tiled=True,
    ).astype(jnp.float32)
    hidden_width = hidden.shape[1]
    gate_grad = grad_sums[:, :hidden_width].astype(jnp.bfloat16)[None]
    up_grad = grad_sums[:, hidden_width : 2 * hidden_width].astype(jnp.bfloat16)[None]
    down_grad = grad_sums[:, 2 * hidden_width :].astype(jnp.bfloat16)[None]
    return (
        layer_out.astype(jnp.bfloat16),
        token_grad.astype(jnp.bfloat16),
        gate_grad,
        up_grad,
        down_grad,
    )


def solution(mesh):
    n_dp, n_expert = mesh.devices.shape
    fine = Mesh(mesh.devices.reshape(n_dp, n_expert // SPLIT, SPLIT), ROWS)
    placed = (
        P(ROWS, None),
        P(ROWS, None, None),
        P(ROWS, None, None),
        P(("yx", "col"), "dp", None),
        P(("yx", "col"), "dp", None),
        P(("yx", "col"), "dp", None),
        P(ROWS, None),
    )
    return jax.shard_map(
        shards,
        mesh=fine,
        in_specs=placed,
        out_specs=(
            P(ROWS, None),
            P(ROWS, None),
            P(("yx", "col"), "dp", None),
            P(("yx", "col"), "dp", None),
            P(("yx", "col"), "dp", None),
        ),
        check_vma=False,
    )
```

profile of v0, /device:TPU:1, one launch (start us, length us, event | category | flops | bytes accessed | tf_op | source)
XLA Modules:
  0.0 441.6 jit_solution(145172162650093640)
XLA Ops:
  11.8 23.6 %all_to_all.10 = bf16[2,16,4,4096]{3,2,0,1:T(4,128)(2,1)} all-to-all(bf16[2,16,4,4096]{3,2,0,1:T(4,128)(2,1)S(1)} %pad_maximum_fusion.3), channel_id=1, replica_groups=mesh['dp'=2,'yx'=16,'col'=8] {'yx'}, dimensions={1} | all-to-all | bytes 2097152 | tf_op jit(solution)/shard_map/all_to_all | solution.py:12
  35.5 3.7 pad_maximum_fusion.2
  39.4 75.8 %all-gather.3.cloned.1.call-done = bf16[2,128,4,4096]{3,2,0,1:T(4,128)(2,1)} async-done(((bf16[2,16,4,4096]{3,2,0,1:T(4,128)(2,1)}), bf16[2,128,4,4096]{3,2,0,1:T(4,128)(2,1)}) %all-gather.3.cloned.1.call-update) | async-done | bytes 8388624 | tf_op jit(solution)/shard_map/all_gather | solution.py:13
  115.2 10.1 %fusion.12 = (bf16[1,128,4,4096]{3,2,0,1:T(4,128)(2,1)}, bf16[1,128,4,4096]{3,2,0,1:T(4,128)(2,1)}) fusion(bf16[2,128,4,4096]{3,2,0,1:T(4,128)(2,1)} %all-gather.3.cloned.1.call-done), kind=kLoop, calls=%fused_computation.39 | loop fusion | bytes 16777216 | tf_op jit(solution)/shard_map/slice | solution.py:37
  125.3 6.9 %squeeze.25 = bf16[512,4096]{1,0:T(8,128)(2,1)} reshape(bf16[1,128,4,4096]{3,2,0,1:T(4,128)(2,1)} %get-tuple-element.26) | data formatting | bytes 8388608 | tf_op jit(solution)/shard_map/squeeze | solution.py:37
  132.3 7.1 %squeeze.29 = bf16[512,4096]{1,0:T(8,128)(2,1)} reshape(bf16[1,128,4,4096]{3,2,0,1:T(4,128)(2,1)} %get-tuple-element.25) | data formatting | bytes 8388608 | tf_op jit(solution)/shard_map/squeeze | solution.py:37
  139.4 69.8 %all-gather.5.cloned.1.call-done = bf16[3,4096,256]{2,1,0:T(8,128)(2,1)} async-done(((bf16[3,2048,256]{2,1,0:T(8,128)(2,1)}), bf16[3,4096,256]{2,1,0:T(8,128)(2,1)}) %all-gather.5.cloned.1.call-update) | async-done | bytes 6291472 | tf_op jit(solution)/shard_map/all_gather | solution.py:33
  209.2 4.2 fusion.3
  213.9 3.6 fusion.5
  217.5 1.4 multiply_convert_fusion.2
  220.2 3.3 fusion
  224.8 6.2 %pad_maximum_fusion = bf16[2,512,4096]{2,1,0:T(8,128)(2,1)} fusion(bf16[1,512,4096]{2,1,0:T(8,128)(2,1)S(1)} %fusion.1, bf16[1,512,4096]{2,1,0:T(8,128)(2,1)} %fusion), kind=kLoop, calls=%fused_computation.4 | loop fusion | flops 4194304 | bytes 16777216 | tf_op jit(solution)/shard_map/stack | solution.py:54
  231.3 3.6 convolution_convert_fusion.2
  238.5 9.5 %pad_maximum_fusion.1 = bf16[4096,768]{0,1:T(8,128)(2,1)} fusion(bf16[4096,256]{0,1:T(8,128)(2,1)S(1)} %convolution_convert_fusion.1, bf16[4096,256]{0,1:T(8,128)(2,1)S(1)} %convolution_convert_fusion.2, bf16[4096,256]{0,1:T(8,128)(2,1)S(1)} %convolution_convert_fusion.3), kind=kLoop, calls=%fused_computation.6 | loop fusion | flops 18874368 | bytes 12582912 | tf_op jit(solution)/shard_map/concatenate | solution.py:58
  248.0 79.6 %reduce-scatter.3.cloned.1.call-done = bf16[2,64,4096]{2,1,0:T(8,128)(2,1)} async-done(((bf16[2,512,4096]{2,1,0:T(8,128)(2,1)}), bf16[2,64,4096]{2,1,0:T(8,128)(2,1)}) %reduce-scatter.3.cloned.1.call-update) | async-done | bytes 1048592 | tf_op jit(solution)/shard_map/reduce_scatter | solution.py:19
  327.7 1.5 reshape.62
  329.1 1.6 copy.38
  330.7 7.1 %all-to-all-start.1 = ((bf16[2,16,4,4096]{3,2,0,1:T(4,128)(2,1)}), bf16[2,16,4,4096]{3,2,0,1:T(4,128)(2,1)S(1)}, u32[]{:S(2)}, u32[]{:S(2)}) async-start(bf16[2,16,4,4096]{3,2,0,1:T(4,128)(2,1)} %copy.38), calls=%async_computation.2 | async-start | bytes 2097152 | tf_op jit(solution)/shard_map/all_to_all | solution.py:21
  337.8 76.7 %reduce-scatter.5.cloned.1.call-done = bf16[2048,768]{0,1:T(8,128)(2,1)} async-done(((bf16[4096,768]{0,1:T(8,128)(2,1)}), bf16[2048,768]{0,1:T(8,128)(2,1)}) %reduce-scatter.5.cloned.1.call-update) | async-done | bytes 3145744 | tf_op jit(solution)/shard_map/reduce_scatter | solution.py:57
  414.5 3.2 slice_bitcast_fusion.9
  417.7 2.3 copy.39
  423.4 3.3 scatter_custom_fusion
  426.7 2.7 convert_element_type.61
  430.9 3.1 scatter_custom_fusion.1
  (50 shorter events, 17.6 us)
Async XLA Ops:
  7.2 1.2 copy-start
  7.2 2.4 copy-start.8
  7.2 2.5 copy-start.2
  7.2 108.0 %all-gather.3.cloned.1.call-start = ((), (), s32[]{:S(2)}) async-start(), calls=%async_computation.4 | async-start | bytes 9437184 | tf_op jit(solution)/shard_map/all_gather | solution.py:13
  10.8 24.7 %copy-start.7 = (bf16[1,2048,256]{2,1,0:T(8,128)(2,1)S(1)}, bf16[1,2048,256]{2,1,0:T(8,128)(2,1)}, u32[]{:S(2)}) copy-start(bf16[1,2048,256]{2,1,0:T(8,128)(2,1)} %param.12) | copy-start | bytes 3145732
  35.4 173.8 %all-gather.5.cloned.1.call-start = ((), (), s32[]{:S(2)}) async-start(), calls=%async_computation.5 | async-start | bytes 9437184 | tf_op jit(solution)/shard_map/all_gather | solution.py:33
  39.2 288.5 %reduce-scatter.3.cloned.1.call-start = ((), (), s32[]{:S(2)}) async-start(), calls=%async_computation.6 | async-start | bytes 9437184 | tf_op jit(solution)/shard_map/reduce_scatter | solution.py:19
  209.2 4.7 %copy-start.3 = (bf16[3,4096,256]{2,1,0:T(8,128)(2,1)S(1)}, bf16[3,4096,256]{2,1,0:T(8,128)(2,1)}, u32[]{:S(2)}) copy-start(bf16[3,4096,256]{2,1,0:T(8,128)(2,1)} %all-gather.5.cloned.1.call-done) | copy-start | bytes 18874372
  213.8 3.6 copy-start.4
  231.0 183.5 %reduce-scatter.5.cloned.1.call-start = ((), (), s32[]{:S(2)}) async-start(), calls=%async_computation.7 | async-start | bytes 9437184 | tf_op jit(solution)/shard_map/reduce_scatter | solution.py:57
  231.2 3.7 copy-start.5
  234.9 2.2 copy-start.6
  330.7 91.8 %all-to-all-start.1 = ((bf16[2,16,4,4096]{3,2,0,1:T(4,128)(2,1)}), bf16[2,16,4,4096]{3,2,0,1:T(4,128)(2,1)S(1)}, u32[]{:S(2)}, u32[]{:S(2)}) async-start(bf16[2,16,4,4096]{3,2,0,1:T(4,128)(2,1)} %copy.38), calls=%async_computation.2 | async-start | bytes 2097152 | tf_op jit(solution)/shard_map/all_to_all | solution.py:21
  429.4 5.7 %copy-start.1 = (bf16[128,4096]{1,0:T(8,128)(2,1)S(1)}, bf16[128,4096]{1,0:T(8,128)(2,1)}, u32[]{:S(2)}) copy-start(bf16[128,4096]{1,0:T(8,128)(2,1)} %param.13) | copy-start | bytes 3145732
Sparse Core Ops, SparseCore 0:
  35.5 79.6 all-gather.2
  117.0 92.1 all-gather.4
  231.1 96.5 reduce-scatter.2
  330.1 84.3 reduce-scatter.4
where the time goes:
time: 442 us
  waiting for transfers between devices  302 us (68%)
  local copies, waits for them, and re-layouts  40.9 us (9%)
  other arithmetic  31.9 us (7%)
  blocking collectives  23.6 us (5%)
  matrix products  21.5 us (5%)
  between operations  14 us (3%)
  starting transfers between devices  7.63 us (2%)
    reduce_scatter x1, waiting for transfers between devices, bring_back(): lax.psum_scatter(partial_value, 'col', scatter_dimension=1, tiled=True)  79.6 us
    reduce_scatter x1, waiting for transfers between devices, shards(): lax.psum_scatter(jnp.concatenate([lax.dot_general(token_rows, gate_rows,...  76.7 us
    all_gather x1, waiting for transfers between devices, send_out(): shared = lax.all_gather(arrived, 'col', axis=1, tiled=True)  75.8 us
    all_gather x1, waiting for transfers between devices, shards(): full = lax.all_gather(weights, 'dp', axis=1, tiled=True)  69.8 us
    all_to_all x1, blocking collectives, send_out(): lax.all_to_all(payload, 'yx', split_axis=1, concat_axis=1, tiled=True)  23.6 us
    squeeze x2, local copies, waits for them, and re-layouts, shards(): token_rows, cot_rows = (both_rows[0], both_rows[1])  14 us
    slice x1, local copies, waits for them, and re-layouts, shards(): token_rows, cot_rows = (both_rows[0], both_rows[1])  10.1 us
    concatenate x1, other arithmetic, shards(): jnp.concatenate([lax.dot_general(token_rows, gate_rows, contract_first, p...  9.54 us
  transfers between devices with their start and end apart: 5, of which 4 were waited for; matrix products, arithmetic and copies ran while one was open for 12% of the time, Pallas kernels for 0%

commit v1 on v0

--- a/solution.py
+++ b/solution.py
@@ -10,7 +10,9 @@
 
 def send_out(payload):
     arrived = lax.all_to_all(payload, "yx", split_axis=1, concat_axis=1, tiled=True)
-    shared = lax.all_gather(arrived, "col", axis=1, tiled=True)
+    shared = jnp.concatenate(
+        lax.all_to_all(jnp.stack([arrived] * lax.axis_size("col")), "col", 0, 0), axis=1
+    )
     return shared.reshape(payload.shape[0], -1, payload.shape[-1])
 
 

time: 442 us -> 557 us (1.26)
  waiting for transfers between devices: 302 us -> 400 us
  starting transfers between devices: 7.63 us -> 18.4 us
  local copies, waits for them, and re-layouts: 40.9 us -> 48.6 us
    all_to_all x0 -> x1, waiting for transfers between devices: none -> 245 us  [send_out(): lax.all_to_all(jnp.stack([arrived] * lax.axis_size('col')), 'col', 0, 0)]
    all_gather x1 -> x0, waiting for transfers between devices: 75.8 us -> none  [send_out(): shared = lax.all_gather(arrived, 'col', axis=1, tiled=True)]
    all_gather x1, waiting for transfers between devices: 69.8 us -> 0.01 us  [shards(): full = lax.all_gather(weights, 'dp', axis=1, tiled=True)]
    all_to_all x0 -> x1, starting transfers between devices: none -> 10.7 us  [send_out(): lax.all_to_all(jnp.stack([arrived] * lax.axis_size('col')), 'col', 0, 0)]
    another operation x0 -> x1, local copies, waits for them, and re-layouts: none -> 7.5 us  [send_out(): jnp.stack([arrived] * lax.axis_size('col'))]
  transfers between devices with their start and end apart: 5 -> 5, of which waited for: 4 -> 3; matrix products, arithmetic and copies ran while one was open for 12% -> 10% of each run, Pallas kernels for 0% -> 0%
where the time goes in v1:
time: 557 us; the launch traced here: 556 us
  waiting for transfers between devices  400 us (72%)
  local copies, waits for them, and re-layouts  48.6 us (9%)
  other arithmetic  30.4 us (5%)
  blocking collectives  23.5 us (4%)
  matrix products  21.5 us (4%)
  starting transfers between devices  18.4 us (3%)
  between operations  14 us (3%)
    all_to_all x1, waiting for transfers between devices, send_out(): lax.all_to_all(jnp.stack([arrived] * lax.axis_size('col')), 'col', 0, 0)  245 us
    reduce_scatter x1, waiting for transfers between devices, bring_back(): lax.psum_scatter(partial_value, 'col', scatter_dimension=1, tiled=True)  77.6 us
    reduce_scatter x1, waiting for transfers between devices, shards(): lax.psum_scatter(jnp.concatenate([lax.dot_general(token_rows, gate_rows,...  77.4 us
    all_to_all x1, blocking collectives, send_out(): lax.all_to_all(payload, 'yx', split_axis=1, concat_axis=1, tiled=True)  23.5 us
    squeeze x2, local copies, waits for them, and re-layouts, shards(): token_rows, cot_rows = (both_rows[0], both_rows[1])  13.8 us
  transfers between devices with their start and end apart: 5, of which 3 were waited for; matrix products, arithmetic and copies ran while one was open for 10% of the time, Pallas kernels for 0%

profile of v1, /device:TPU:1, one launch (start us, length us, event | category | flops | bytes accessed | tf_op | source)
XLA Modules:
  0.0 556.5 jit_solution(17178390444024709563)
XLA Ops:
  11.8 23.5 %all_to_all.15 = bf16[2,16,4,4096]{3,2,0,1:T(4,128)(2,1)S(1)} all-to-all(bf16[2,16,4,4096]{3,2,0,1:T(4,128)(2,1)S(1)} %pad_maximum_fusion.3), channel_id=1, replica_groups=mesh['dp'=2,'yx'=16,'col'=8] {'yx'}, dimensions={1} | all-to-all | bytes 2097152 | tf_op jit(solution)/shard_map/all_to_all | solution.py:12
  35.7 7.5 %stack.14 = bf16[8,2,16,4,4096]{4,3,2,1,0:T(4,128)(2,1)} broadcast(bf16[2,16,4,4096]{3,2,1,0:T(4,128)(2,1)S(1)} %copy.29), dimensions={1,2,3,4} | broadcast | bytes 9437184 | tf_op jit(solution)/shard_map/stack | solution.py:14
  43.2 10.7 %all-to-all-start.1 = ((bf16[8,2,16,4,4096]{4,3,2,1,0:T(4,128)(2,1)}), bf16[8,2,16,4,4096]{4,3,2,1,0:T(4,128)(2,1)}, u32[]{:S(2)}, u32[]{:S(2)}) async-start(bf16[8,2,16,4,4096]{4,3,2,1,0:T(4,128)(2,1)} %stack.14), calls=%async_computation.1 | async-start | bytes 16777216 | tf_op jit(solution)/shard_map/all_to_all | solution.py:14
  53.9 2.1 pad_maximum_fusion.2
  56.3 245.2 %all-to-all-done.1 = bf16[8,2,16,4,4096]{4,3,2,1,0:T(4,128)(2,1)} async-done(((bf16[8,2,16,4,4096]{4,3,2,1,0:T(4,128)(2,1)}), bf16[8,2,16,4,4096]{4,3,2,1,0:T(4,128)(2,1)}, u32[]{:S(2)}, u32[]{:S(2)}) %all-to-all-start.1) | async-done | bytes 8388640 | tf_op jit(solution)/shard_map/all_to_all | solution.py:14
  301.5 10.0 %fusion.12 = (bf16[1,8,16,4,4096]{4,3,2,0,1:T(4,128)(2,1)}, bf16[1,8,16,4,4096]{4,3,2,0,1:T(4,128)(2,1)}) fusion(bf16[2,8,16,4,4096]{4,3,2,0,1:T(4,128)(2,1)} %bitcast.4), kind=kLoop, calls=%fused_computation.39 | loop fusion | bytes 16777216 | tf_op jit(solution)/shard_map/slice | solution.py:39
  311.5 6.9 %squeeze.25 = bf16[512,4096]{1,0:T(8,128)(2,1)} reshape(bf16[1,8,16,4,4096]{4,3,2,0,1:T(4,128)(2,1)} %get-tuple-element.21) | data formatting | bytes 8388608 | tf_op jit(solution)/shard_map/squeeze | solution.py:39
  318.4 6.9 %squeeze.29 = bf16[512,4096]{1,0:T(8,128)(2,1)} reshape(bf16[1,8,16,4,4096]{4,3,2,0,1:T(4,128)(2,1)} %get-tuple-element.20) | data formatting | bytes 8388608 | tf_op jit(solution)/shard_map/squeeze | solution.py:39
  325.3 4.2 fusion.3
  330.0 3.6 fusion.5
  336.3 3.2 fusion
  340.9 6.2 %pad_maximum_fusion = bf16[2,512,4096]{2,1,0:T(8,128)(2,1)} fusion(bf16[1,512,4096]{2,1,0:T(8,128)(2,1)S(1)} %fusion.1, bf16[1,512,4096]{2,1,0:T(8,128)(2,1)} %fusion), kind=kLoop, calls=%fused_computation.4 | loop fusion | flops 4194304 | bytes 16777216 | tf_op jit(solution)/shard_map/stack | solution.py:56
  347.4 3.6 convolution_convert_fusion.2
  354.6 9.6 %pad_maximum_fusion.1 = bf16[4096,768]{0,1:T(8,128)(2,1)} fusion(bf16[4096,256]{0,1:T(8,128)(2,1)S(1)} %convolution_convert_fusion.1, bf16[4096,256]{0,1:T(8,128)(2,1)S(1)} %convolution_convert_fusion.2, bf16[4096,256]{0,1:T(8,128)(2,1)S(1)} %convolution_convert_fusion.3), kind=kLoop, calls=%fused_computation.6 | loop fusion | flops 18874368 | bytes 12582912 | tf_op jit(solution)/shard_map/concatenate | solution.py:60
  364.1 77.6 %reduce-scatter.3.cloned.1.call-done = bf16[2,64,4096]{2,1,0:T(8,128)(2,1)} async-done(((bf16[2,512,4096]{2,1,0:T(8,128)(2,1)}), bf16[2,64,4096]{2,1,0:T(8,128)(2,1)}) %reduce-scatter.3.cloned.1.call-update) | async-done | bytes 1048592 | tf_op jit(solution)/shard_map/reduce_scatter | solution.py:21
  441.7 1.5 reshape.67
  443.2 1.6 copy.30
  444.8 7.2 %all-to-all-start.2 = ((bf16[2,16,4,4096]{3,2,0,1:T(4,128)(2,1)}), bf16[2,16,4,4096]{3,2,0,1:T(4,128)(2,1)S(1)}, u32[]{:S(2)}, u32[]{:S(2)}) async-start(bf16[2,16,4,4096]{3,2,0,1:T(4,128)(2,1)} %copy.30), calls=%async_computation.3 | async-start | bytes 2097152 | tf_op jit(solution)/shard_map/all_to_all | solution.py:23
  452.0 77.4 %reduce-scatter.5.cloned.1.call-done = bf16[2048,768]{0,1:T(8,128)(2,1)} async-done(((bf16[4096,768]{0,1:T(8,128)(2,1)}), bf16[2048,768]{0,1:T(8,128)(2,1)}) %reduce-scatter.5.cloned.1.call-update) | async-done | bytes 3145744 | tf_op jit(solution)/shard_map/reduce_scatter | solution.py:59
  529.4 3.2 slice_bitcast_fusion.9
  532.5 2.3 copy.31
  538.3 3.3 scatter_custom_fusion
  541.6 2.7 convert_element_type.61
  545.8 3.1 scatter_custom_fusion.1
  (55 shorter events, 19.4 us)
Async XLA Ops:
  7.2 1.2 copy-start
  7.2 2.4 copy-start.10
  7.2 2.5 copy-start.2
  43.2 10.7 %copy-start.7 = (bf16[1,2048,256]{2,1,0:T(8,128)(2,1)S(1)}, bf16[1,2048,256]{2,1,0:T(8,128)(2,1)}, u32[]{:S(2)}) copy-start(bf16[1,2048,256]{2,1,0:T(8,128)(2,1)} %param.12) | copy-start | bytes 3145732
  43.2 10.7 %copy-start.8 = (bf16[1,2048,256]{2,1,0:T(8,128)(2,1)S(1)}, bf16[1,2048,256]{2,1,0:T(8,128)(2,1)}, u32[]{:S(2)}) copy-start(bf16[1,2048,256]{2,1,0:T(8,128)(2,1)} %param.11) | copy-start | bytes 3145732
  43.2 10.7 %copy-start.9 = (bf16[1,2048,256]{2,1,0:T(8,128)(2,1)S(1)}, bf16[1,2048,256]{2,1,0:T(8,128)(2,1)}, u32[]{:S(2)}) copy-start(bf16[1,2048,256]{2,1,0:T(8,128)(2,1)} %param.10) | copy-start | bytes 3145732
  43.2 258.3 %all-to-all-start.1 = ((bf16[8,2,16,4,4096]{4,3,2,1,0:T(4,128)(2,1)}), bf16[8,2,16,4,4096]{4,3,2,1,0:T(4,128)(2,1)}, u32[]{:S(2)}, u32[]{:S(2)}) async-start(bf16[8,2,16,4,4096]{4,3,2,1,0:T(4,128)(2,1)} %stack.14), calls=%async_computation.1 | async-start | bytes 16777216 | tf_op jit(solution)/shard_map/all_to_all | solution.py:14
  53.9 271.4 %all-gather.2.cloned.1.call-start = ((), (), s32[]{:S(2)}) async-start(), calls=%async_computation.5 | async-start | bytes 9437184 | tf_op jit(solution)/shard_map/all_gather | solution.py:35
  56.1 385.6 %reduce-scatter.3.cloned.1.call-start = ((), (), s32[]{:S(2)}) async-start(), calls=%async_computation.6 | async-start | bytes 9437184 | tf_op jit(solution)/shard_map/reduce_scatter | solution.py:21
  325.3 4.7 copy-start.3
  330.0 3.6 copy-start.4
  347.1 182.3 %reduce-scatter.5.cloned.1.call-start = ((), (), s32[]{:S(2)}) async-start(), calls=%async_computation.7 | async-start | bytes 9437184 | tf_op jit(solution)/shard_map/reduce_scatter | solution.py:59
  347.4 3.7 copy-start.5
  351.0 2.2 copy-start.6
  444.8 92.6 %all-to-all-start.2 = ((bf16[2,16,4,4096]{3,2,0,1:T(4,128)(2,1)}), bf16[2,16,4,4096]{3,2,0,1:T(4,128)(2,1)S(1)}, u32[]{:S(2)}, u32[]{:S(2)}) async-start(bf16[2,16,4,4096]{3,2,0,1:T(4,128)(2,1)} %copy.30), calls=%async_computation.3 | async-start | bytes 2097152 | tf_op jit(solution)/shard_map/all_to_all | solution.py:23
  544.3 5.7 %copy-start.1 = (bf16[128,4096]{1,0:T(8,128)(2,1)S(1)}, bf16[128,4096]{1,0:T(8,128)(2,1)}, u32[]{:S(2)}) copy-start(bf16[128,4096]{1,0:T(8,128)(2,1)} %param.13) | copy-start | bytes 3145732
Sparse Core Ops, SparseCore 0:
  56.5 219.7 all-gather.1
  347.2 94.4 reduce-scatter.2
  444.3 85.0 reduce-scatter.4
